TPU v7x, 256 devices: a whole 4x4x8 slice. The times are simulated.
256 devices in a mesh: roll: 4 (over z_lo, core), mach: 16 (over y, x), cross: 4 (over z_hi).
Axes of the slice: x: 4, y: 4, z: 8 (z_hi: 4, z_lo: 2; z = z_hi * 2 + z_lo), core: 2. Of those that a mesh axis runs over, the one named last changes fastest.
Arguments:
- density: bfloat16 [128, 4096, 2048], P('roll', 'mach', 'cross'), may hold values from 0 to 1
- roll_start: float32 [32, 128], P(None, 'roll'), may hold values from 0.05 to 1
- mach_factor: bfloat16 [32, 4096], P(None, 'mach'), may hold values from 0.0099487305 to 1
- cross_factor: bfloat16 [32, 2048], P(None, 'cross'), may hold values from 0.0099487305 to 1
Outputs:
- roll_factor: float32 [32, 128], P(None, 'roll')
- mode_two: float32 [32, 4096], P(None, ('mach', 'cross'))
All inputs are finite; a program needn't handle non-finite values.
Results may differ from a plain program's by a relative error of at most 0.0003.
Values sent between devices are 32-bit elements; how exact they have to be, the bound alone decides.
A program may use at most 64 MiB of HBM per device.

v0:
```python
import jax
import jax.numpy as jnp
from jax import lax
from jax.sharding import PartitionSpec as P


def hals_rows(roll_rows, mttkrp, gram):

    def column_step(column, rows):
        column = jnp.asarray(column).astype(jnp.int32)
        gram_row = lax.dynamic_slice_in_dim(gram, column, 1, 0)
        diag_entry = lax.dynamic_slice_in_dim(gram_row, column, 1, 1)
        current = lax.dynamic_slice_in_dim(rows, column, 1, 0)
        target = lax.dynamic_slice_in_dim(mttkrp, column, 1, 0)
        mixed = jnp.dot(gram_row, rows, precision=lax.Precision.HIGHEST)
        updated = jnp.maximum(current + (target - mixed) / diag_entry, 0.0)
        return lax.dynamic_update_slice_in_dim(rows, updated, column, 0)

    return lax.fori_loop(0, roll_rows.shape[0], column_step, roll_rows)


def local(density, roll_start, mach_factor, cross_factor):
    rolls_here, bins_here, cross_here = density.shape
    rank = cross_factor.shape[0]
    flat = density.reshape(rolls_here * bins_here, cross_here)
    partial_value = lax.dot_general(
        cross_factor, flat, (((1,), (1,)), ((), ())), preferred_element_type=jnp.float32
    )
    partial_value = partial_value.reshape(rank, rolls_here, bins_here)
    local_terms = jnp.einsum(
        "rij,rj->ri",
        partial_value,
        mach_factor.astype(jnp.float32),
        precision=lax.Precision.HIGHEST,
    )
    local_mach = jnp.dot(mach_factor, mach_factor.T, preferred_element_type=jnp.float32)
    local_cross = jnp.dot(cross_factor, cross_factor.T, preferred_element_type=jnp.float32)
    mttkrp = lax.psum(local_terms, ("mach", "cross"))
    gram_mach = lax.psum(local_mach, "mach")
    gram_cross = lax.psum(local_cross, "cross")
    gram = gram_mach * gram_cross
    roll_factor = hals_rows(roll_start, mttkrp, gram)
    term = jnp.einsum("rij,ri->rj", partial_value, roll_factor, precision=lax.Precision.HIGHEST)
    whole = lax.psum(term, ("roll", "cross"))
    span = whole.shape[1] // lax.axis_size("cross")
    total = lax.dynamic_slice_in_dim(whole, lax.axis_index("cross") * span, span, 1)
    all_rolls = rolls_here * lax.axis_size("roll")
    all_cross = cross_here * lax.axis_size("cross")
    scale = rank / (all_rolls * all_cross)
    mode_two = total * scale
    return (roll_factor, mode_two)


def solution(mesh):
    in_specs = (P("roll", "mach", "cross"), P(None, "roll"), P(None, "mach"), P(None, "cross"))
    out_specs = (P(None, "roll"), P(None, ("mach", "cross")))
    return jax.shard_map(local, mesh=mesh, in_specs=in_specs, out_specs=out_specs, check_vma=False)
```

profile of v0, /device:TPU:1, one launch (start us, length us, event | category | flops | bytes accessed | tf_op | source)
XLA Modules:
  0.0 584.9 jit_solution(14968535453906031717)
XLA Ops:
  1.4 5.9 %fusion.9 = f32[32,32,256]{2,0,1:T(8,128)S(1)} fusion(bf16[32,256,512]{2,1,0:T(8,128)(2,1)} %param.6, bf16[32,512]{1,0:T(8,128)(2,1)S(1)} %copy-done), kind=kOutput, calls=%fused_computation.12 | convolution fusion | flops 268435456 | bytes 9469952 | tf_op jit(solution)/shard_map/dot_general | solution.py:26
  7.3 1.2 fusion.7
  8.5 327.1 %psum.28 = f32[32,32]{1,0:T(8,128)S(1)} all-reduce(f32[32,32]{1,0:T(8,128)S(1)} %bitcast.34), channel_id=1, replica_groups=mesh['roll'=4,'mach'=16,'cross'=4] {'mach','cross'}, use_global_device_ids=true, to_apply=%region_2.0 | all-reduce | flops 1024 | bytes 8192 | tf_op jit(solution)/shard_map/psum | solution.py:38
  335.7 56.2 %psum.29 = f32[32,32]{1,0:T(8,128)S(1)} all-reduce(f32[32,32]{1,0:T(8,128)S(1)} %fusion.12), channel_id=1, replica_groups=mesh['roll'=4,'mach'=16,'cross'=4] {'mach'}, use_global_device_ids=true, to_apply=%region_0.0 | all-reduce | flops 1024 | bytes 8192 | tf_op jit(solution)/shard_map/psum | solution.py:39
  392.0 12.7 %psum.30 = f32[32,32]{1,0:T(8,128)S(1)} all-reduce(f32[32,32]{1,0:T(8,128)S(1)} %fusion.13), channel_id=1, replica_groups=mesh['roll'=4,'mach'=16,'cross'=4] {'cross'}, use_global_device_ids=true, to_apply=%region_1.0 | all-reduce | flops 1024 | bytes 8192 | tf_op jit(solution)/shard_map/psum | solution.py:40
  404.7 45.2 %while.16 = (s32[]{:T(128)}, f32[32,32]{1,0:T(8,128)S(1)}, f32[32,32]{1,0:T(8,128)S(1)}, f32[32,32]{1,0:T(8,128)S(1)}, s32[]{:T(128)}, /*index=5*/s32[]{:T(128)}, s32[]{:T(128)}) while((s32[]{:T(128)}, f32[32,32]{1,0:T(8,128)S(1)}, f32[32,32]{1,0:T(8,128)S(1)}, f32[32,32]{1,0:T(8,128)S(1)}, s32[]{:T(128)}, /*index=5*/s32[]{:T(128)}, ...), condition=%wide.region_4.0_spmd, body=%wide.region_3.0_spmd.sunk | while | flops 12419 | bytes 19449 | solution.py:19
  405.3 0.8 fusion.26
  406.7 0.8 fusion.26
  408.1 0.8 fusion.26
  409.6 0.8 fusion.26
  411.0 0.8 fusion.26
  412.4 0.8 fusion.26
  413.8 0.8 fusion.26
  415.2 0.8 fusion.26
  416.6 0.8 fusion.26
  418.0 0.8 fusion.26
  419.4 0.8 fusion.26
  420.8 0.8 fusion.26
  422.3 0.8 fusion.26
  423.7 0.8 fusion.26
  425.1 0.8 fusion.26
  426.5 0.8 fusion.26
  429.3 0.8 fusion.26
  430.7 0.8 fusion.26
  432.1 0.8 fusion.26
  433.6 0.8 fusion.26
  435.0 0.8 fusion.26
  436.4 0.8 fusion.26
  437.8 0.8 fusion.26
  439.2 0.8 fusion.26
  449.9 1.3 fusion.5
  451.2 133.1 %psum.31 = f32[32,256]{1,0:T(8,128)S(1)} all-reduce(f32[32,256]{1,0:T(8,128)S(1)} %bitcast.33), channel_id=1, replica_groups=mesh['roll'=4,'mach'=16,'cross'=4] {'roll','cross'}, use_global_device_ids=true, to_apply=%region_5.0 | all-reduce | flops 8192 | bytes 65536 | tf_op jit(solution)/shard_map/psum | solution.py:44
  (85 shorter events, 27.6 us)
Async XLA Ops:
  0.6 0.8 copy-start
  0.6 404.1 %copy-start.2 = (f32[32,32]{1,0:T(8,128)S(1)}, f32[32,32]{1,0:T(8,128)}, u32[]{:S(2)}) copy-start(f32[32,32]{1,0:T(8,128)} %param.7) | copy-start | bytes 12292
  0.7 6.6 %copy-start.3 = (bf16[32,256]{1,0:T(8,128)(2,1)S(1)}, bf16[32,256]{1,0:T(8,128)(2,1)}, u32[]{:S(2)}) copy-start(bf16[32,256]{1,0:T(8,128)(2,1)} %param.8) | copy-start | bytes 49156
  449.9 135.0 %copy-start.1 = (f32[32,32]{1,0:T(8,128)}, f32[32,32]{1,0:T(8,128)S(1)}, u32[]{:S(2)}) copy-start(f32[32,32]{1,0:T(8,128)S(1)} %get-tuple-element.124) | copy-start | bytes 12292
where the time goes:
time: 585 us
  blocking collectives  529 us (90%)
  matrix products  33.6 us (6%)
  local copies, waits for them, and re-layouts  20.4 us (3%)
    psum x1, blocking collectives, local(): mttkrp = lax.psum(local_terms, ('mach', 'cross'))  327 us
    psum x1, blocking collectives, local(): whole = lax.psum(term, ('roll', 'cross'))  133 us
    psum x1, blocking collectives, local(): gram_mach = lax.psum(local_mach, 'mach')  56.2 us
    dot_general x32, matrix products, column_step(): mixed = jnp.dot(gram_row, rows, precision=lax.Precision.HIGHEST)  25 us
    dynamic_slice x32, local copies, waits for them, and re-layouts, column_step(): diag_entry = lax.dynamic_slice_in_dim(gram_row, column, 1, 1)  18.8 us
    psum x1, blocking collectives, local(): gram_cross = lax.psum(local_cross, 'cross')  12.7 us

commit v1 on v0

--- a/solution.py
+++ b/solution.py
@@ -35,7 +35,7 @@
     )
     local_mach = jnp.dot(mach_factor, mach_factor.T, preferred_element_type=jnp.float32)
     local_cross = jnp.dot(cross_factor, cross_factor.T, preferred_element_type=jnp.float32)
-    mttkrp = lax.psum(local_terms, ("mach", "cross"))
+    mttkrp = lax.psum(lax.psum(local_terms, "cross"), "mach")
     gram_mach = lax.psum(local_mach, "mach")
     gram_cross = lax.psum(local_cross, "cross")
     gram = gram_mach * gram_cross

time: 585 us -> 214 us (0.37)
  blocking collectives: 529 us -> 158 us
    psum x3 -> x2, blocking collectives: 396 us -> 80.3 us  [local(): mttkrp = lax.psum(lax.psum(local_terms, 'cross'), 'mach')]
    psum x1, blocking collectives: 133 us -> 77.6 us  [local(): whole = lax.psum(term, ('roll', 'cross'))]
where the time goes in v1:
time: 214 us
  blocking collectives  158 us (74%)
  matrix products  33.6 us (16%)
  local copies, waits for them, and re-layouts  20.4 us (10%)
    psum x2, blocking collectives, local(): mttkrp = lax.psum(lax.psum(local_terms, 'cross'), 'mach')  80.3 us
    psum x1, blocking collectives, local(): whole = lax.psum(term, ('roll', 'cross'))  77.6 us
    dot_general x32, matrix products, column_step(): mixed = jnp.dot(gram_row, rows, precision=lax.Precision.HIGHEST)  25 us
    dynamic_slice x32, local copies, waits for them, and re-layouts, column_step(): diag_entry = lax.dynamic_slice_in_dim(gram_row, column, 1, 1)  18.8 us
    dot_general x1, matrix products, local(): lax.dot_general(cross_factor, flat, (((1,), (1,)), ((), ())), preferred_e...  5.9 us

profile of v1, /device:TPU:1, one launch (start us, length us, event | category | flops | bytes accessed | tf_op | source)
XLA Modules:
  0.0 213.8 jit_solution(8567797768996771899)
XLA Ops:
  1.4 5.9 %fusion.9 = f32[32,32,256]{2,0,1:T(8,128)S(1)} fusion(bf16[32,256,512]{2,1,0:T(8,128)(2,1)} %param.6, bf16[32,512]{1,0:T(8,128)(2,1)S(1)} %copy-done), kind=kOutput, calls=%fused_computation.12 | convolution fusion | flops 268435456 | bytes 9469952 | tf_op jit(solution)/shard_map/dot_general | solution.py:26
  7.3 1.2 fusion.7
  8.6 19.5 %all-reduce.1 = (f32[32,32]{1,0:T(8,128)S(1)}, f32[32,32]{1,0:T(8,128)S(1)}) all-reduce(f32[32,32]{1,0:T(8,128)S(1)} %bitcast.34, f32[32,32]{1,0:T(8,128)S(1)} %fusion.13), channel_id=1, replica_groups=mesh['roll'=4,'mach'=16,'cross'=4] {'cross'}, use_global_device_ids=true, to_apply=%region_2.0 | all-reduce | flops 2048 | bytes 16384 | tf_op jit(solution)/shard_map/psum | solution.py:38
  28.2 60.8 %all-reduce = (f32[32,32]{1,0:T(8,128)S(1)}, f32[32,32]{1,0:T(8,128)S(1)}) all-reduce(f32[32,32]{1,0:T(8,128)S(1)} %get-tuple-element.137, f32[32,32]{1,0:T(8,128)S(1)} %fusion.12), channel_id=1, replica_groups=mesh['roll'=4,'mach'=16,'cross'=4] {'mach'}, use_global_device_ids=true, to_apply=%region_3.0 | all-reduce | flops 2048 | bytes 16384 | tf_op jit(solution)/shard_map/psum | solution.py:38
  89.0 45.2 %while.16 = (s32[]{:T(128)}, f32[32,32]{1,0:T(8,128)S(1)}, f32[32,32]{1,0:T(8,128)S(1)}, f32[32,32]{1,0:T(8,128)S(1)}, s32[]{:T(128)}, /*index=5*/s32[]{:T(128)}, s32[]{:T(128)}) while((s32[]{:T(128)}, f32[32,32]{1,0:T(8,128)S(1)}, f32[32,32]{1,0:T(8,128)S(1)}, f32[32,32]{1,0:T(8,128)S(1)}, s32[]{:T(128)}, /*index=5*/s32[]{:T(128)}, ...), condition=%wide.region_5.0_spmd, body=%wide.region_4.0_spmd.sunk | while | flops 12419 | bytes 19949 | solution.py:19
  89.6 0.8 fusion.26
  91.0 0.8 fusion.26
  92.4 0.8 fusion.26
  93.8 0.8 fusion.26
  95.3 0.8 fusion.26
  96.7 0.8 fusion.26
  98.1 0.8 fusion.26
  99.5 0.8 fusion.26
  100.9 0.8 fusion.26
  102.3 0.8 fusion.26
  103.7 0.8 fusion.26
  106.5 0.8 fusion.26
  108.0 0.8 fusion.26
  109.4 0.8 fusion.26
  110.8 0.8 fusion.26
  112.2 0.8 fusion.26
  113.6 0.8 fusion.26
  115.0 0.8 fusion.26
  116.4 0.8 fusion.26
  117.8 0.8 fusion.26
  119.3 0.8 fusion.26
  120.7 0.8 fusion.26
  122.1 0.8 fusion.26
  123.5 0.8 fusion.26
  124.9 0.8 fusion.26
  134.2 1.3 fusion.5
  135.5 77.6 %psum.39 = f32[32,256]{1,0:T(8,128)S(1)} all-reduce(f32[32,256]{1,0:T(8,128)S(1)} %bitcast.33), channel_id=1, replica_groups=mesh['roll'=4,'mach'=16,'cross'=4] {'roll','cross'}, use_global_device_ids=true, to_apply=%region_6.0 | all-reduce | flops 8192 | bytes 65536 | tf_op jit(solution)/shard_map/psum | solution.py:44
  (84 shorter events, 26.8 us)
Async XLA Ops:
  0.6 0.8 copy-start
  0.6 6.7 %copy-start.3 = (bf16[32,256]{1,0:T(8,128)(2,1)S(1)}, bf16[32,256]{1,0:T(8,128)(2,1)}, u32[]{:S(2)}) copy-start(bf16[32,256]{1,0:T(8,128)(2,1)} %param.8) | copy-start | bytes 49156
  0.7 88.3 %copy-start.2 = (f32[32,32]{1,0:T(8,128)S(1)}, f32[32,32]{1,0:T(8,128)}, u32[]{:S(2)}) copy-start(f32[32,32]{1,0:T(8,128)} %param.7) | copy-start | bytes 12292
  134.2 79.6 %copy-start.1 = (f32[32,32]{1,0:T(8,128)}, f32[32,32]{1,0:T(8,128)S(1)}, u32[]{:S(2)}) copy-start(f32[32,32]{1,0:T(8,128)S(1)} %get-tuple-element.124) | copy-start | bytes 12292

commit v2 on v0

--- a/solution.py
+++ b/solution.py
@@ -41,7 +41,7 @@
     gram = gram_mach * gram_cross
     roll_factor = hals_rows(roll_start, mttkrp, gram)
     term = jnp.einsum("rij,ri->rj", partial_value, roll_factor, precision=lax.Precision.HIGHEST)
-    whole = lax.psum(term, ("roll", "cross"))
+    whole = lax.psum(lax.psum(term, "roll"), "cross")
     span = whole.shape[1] // lax.axis_size("cross")
     total = lax.dynamic_slice_in_dim(whole, lax.axis_index("cross") * span, span, 1)
     all_rolls = rolls_here * lax.axis_size("roll")

time: 585 us -> 552 us (0.944)
  blocking collectives: 529 us -> 493 us
    psum x1 -> x2, blocking collectives: 133 us -> 96.9 us  [local(): whole = lax.psum(lax.psum(term, 'roll'), 'cross')]
where the time goes in v2:
time: 552 us; the launch traced here: 549 us
  blocking collectives  493 us (89%)
  matrix products  33.6 us (6%)
  local copies, waits for them, and re-layouts  20.4 us (4%)
    psum x1, blocking collectives, local(): mttkrp = lax.psum(local_terms, ('mach', 'cross'))  327 us
    psum x2, blocking collectives, local(): whole = lax.psum(lax.psum(term, 'roll'), 'cross')  96.9 us
    psum x1, blocking collectives, local(): gram_mach = lax.psum(local_mach, 'mach')  56.2 us
    dot_general x32, matrix products, column_step(): mixed = jnp.dot(gram_row, rows, precision=lax.Precision.HIGHEST)  25 us
    dynamic_slice x32, local copies, waits for them, and re-layouts, column_step(): diag_entry = lax.dynamic_slice_in_dim(gram_row, column, 1, 1)  18.8 us
    psum x1, blocking collectives, local(): gram_cross = lax.psum(local_cross, 'cross')  12.7 us

profile of v2, /device:TPU:1, one launch (start us, length us, event | category | flops | bytes accessed | tf_op | source)
XLA Modules:
  0.0 548.8 jit_solution(7887763289000505743)
XLA Ops:
  1.4 5.9 %fusion.9 = f32[32,32,256]{2,0,1:T(8,128)S(1)} fusion(bf16[32,256,512]{2,1,0:T(8,128)(2,1)} %param.6, bf16[32,512]{1,0:T(8,128)(2,1)S(1)} %copy-done), kind=kOutput, calls=%fused_computation.12 | convolution fusion | flops 268435456 | bytes 9469952 | tf_op jit(solution)/shard_map/dot_general | solution.py:26
  7.3 1.2 fusion.7
  8.5 327.1 %psum.35 = f32[32,32]{1,0:T(8,128)S(1)} all-reduce(f32[32,32]{1,0:T(8,128)S(1)} %bitcast.34), channel_id=1, replica_groups=mesh['roll'=4,'mach'=16,'cross'=4] {'mach','cross'}, use_global_device_ids=true, to_apply=%region_2.0 | all-reduce | flops 1024 | bytes 8192 | tf_op jit(solution)/shard_map/psum | solution.py:38
  335.7 56.2 %psum.36 = f32[32,32]{1,0:T(8,128)S(1)} all-reduce(f32[32,32]{1,0:T(8,128)S(1)} %fusion.12), channel_id=1, replica_groups=mesh['roll'=4,'mach'=16,'cross'=4] {'mach'}, use_global_device_ids=true, to_apply=%region_0.0 | all-reduce | flops 1024 | bytes 8192 | tf_op jit(solution)/shard_map/psum | solution.py:39
  392.0 12.7 %psum.37 = f32[32,32]{1,0:T(8,128)S(1)} all-reduce(f32[32,32]{1,0:T(8,128)S(1)} %fusion.13), channel_id=1, replica_groups=mesh['roll'=4,'mach'=16,'cross'=4] {'cross'}, use_global_device_ids=true, to_apply=%region_1.0 | all-reduce | flops 1024 | bytes 8192 | tf_op jit(solution)/shard_map/psum | solution.py:40
  404.7 45.2 %while.16 = (s32[]{:T(128)}, f32[32,32]{1,0:T(8,128)S(1)}, f32[32,32]{1,0:T(8,128)S(1)}, f32[32,32]{1,0:T(8,128)S(1)}, s32[]{:T(128)}, /*index=5*/s32[]{:T(128)}, s32[]{:T(128)}) while((s32[]{:T(128)}, f32[32,32]{1,0:T(8,128)S(1)}, f32[32,32]{1,0:T(8,128)S(1)}, f32[32,32]{1,0:T(8,128)S(1)}, s32[]{:T(128)}, /*index=5*/s32[]{:T(128)}, ...), condition=%wide.region_4.0_spmd, body=%wide.region_3.0_spmd.sunk | while | flops 12419 | bytes 19449 | solution.py:19
  405.3 0.8 fusion.26
  406.7 0.8 fusion.26
  408.1 0.8 fusion.26
  409.6 0.8 fusion.26
  411.0 0.8 fusion.26
  412.4 0.8 fusion.26
  413.8 0.8 fusion.26
  415.2 0.8 fusion.26
  416.6 0.8 fusion.26
  418.0 0.8 fusion.26
  419.4 0.8 fusion.26
  420.8 0.8 fusion.26
  422.3 0.8 fusion.26
  423.7 0.8 fusion.26
  425.1 0.8 fusion.26
  426.5 0.8 fusion.26
  429.3 0.8 fusion.26
  430.7 0.8 fusion.26
  432.1 0.8 fusion.26
  433.6 0.8 fusion.26
  435.0 0.8 fusion.26
  436.4 0.8 fusion.26
  437.8 0.8 fusion.26
  449.9 1.3 fusion.5
  451.2 81.9 %psum.38 = f32[32,256]{1,0:T(8,128)S(1)} all-reduce(f32[32,256]{1,0:T(8,128)S(1)} %bitcast.33), channel_id=1, replica_groups=mesh['roll'=4,'mach'=16,'cross'=4] {'roll'}, use_global_device_ids=true, to_apply=%region_5.0 | all-reduce | flops 8192 | bytes 65536 | tf_op jit(solution)/shard_map/psum | solution.py:44
  533.0 15.1 %psum.39 = f32[32,256]{1,0:T(8,128)S(1)} all-reduce(f32[32,256]{1,0:T(8,128)S(1)} %psum.38), channel_id=1, replica_groups=mesh['roll'=4,'mach'=16,'cross'=4] {'cross'}, use_global_device_ids=true, to_apply=%region_6.0 | all-reduce | flops 8192 | bytes 65536 | tf_op jit(solution)/shard_map/psum | solution.py:44
  (86 shorter events, 28.4 us)
Async XLA Ops:
  0.6 0.8 copy-start
  0.6 404.1 %copy-start.2 = (f32[32,32]{1,0:T(8,128)S(1)}, f32[32,32]{1,0:T(8,128)}, u32[]{:S(2)}) copy-start(f32[32,32]{1,0:T(8,128)} %param.7) | copy-start | bytes 12292
  0.7 6.6 %copy-start.3 = (bf16[32,256]{1,0:T(8,128)(2,1)S(1)}, bf16[32,256]{1,0:T(8,128)(2,1)}, u32[]{:S(2)}) copy-start(bf16[32,256]{1,0:T(8,128)(2,1)} %param.8) | copy-start | bytes 49156
  449.9 98.9 %copy-start.1 = (f32[32,32]{1,0:T(8,128)}, f32[32,32]{1,0:T(8,128)S(1)}, u32[]{:S(2)}) copy-start(f32[32,32]{1,0:T(8,128)S(1)} %get-tuple-element.124) | copy-start | bytes 12292

commit v3 on v0

--- a/solution.py
+++ b/solution.py
@@ -41,7 +41,7 @@
     gram = gram_mach * gram_cross
     roll_factor = hals_rows(roll_start, mttkrp, gram)
     term = jnp.einsum("rij,ri->rj", partial_value, roll_factor, precision=lax.Precision.HIGHEST)
-    whole = lax.psum(term, ("roll", "cross"))
+    whole = jnp.sum(lax.all_gather(term, ("roll", "cross")), axis=0)
     span = whole.shape[1] // lax.axis_size("cross")
     total = lax.dynamic_slice_in_dim(whole, lax.axis_index("cross") * span, span, 1)
     all_rolls = rolls_here * lax.axis_size("roll")

time: 585 us -> 558 us (0.954)
  blocking collectives: 529 us -> 502 us
    psum x1 -> x0, blocking collectives: 133 us -> none  [local(): whole = lax.psum(term, ('roll', 'cross'))]
    all_gather x0 -> x1, blocking collectives: none -> 106 us  [local(): whole = jnp.sum(lax.all_gather(term, ('roll', 'cross')), axis=0)]
where the time goes in v3:
time: 558 us
  blocking collectives  502 us (90%)
  matrix products  33.6 us (6%)
  local copies, waits for them, and re-layouts  20.4 us (4%)
    psum x1, blocking collectives, local(): mttkrp = lax.psum(local_terms, ('mach', 'cross'))  327 us
    all_gather x1, blocking collectives, local(): whole = jnp.sum(lax.all_gather(term, ('roll', 'cross')), axis=0)  106 us
    psum x1, blocking collectives, local(): gram_mach = lax.psum(local_mach, 'mach')  56.2 us
    dot_general x32, matrix products, column_step(): mixed = jnp.dot(gram_row, rows, precision=lax.Precision.HIGHEST)  25 us
    dynamic_slice x32, local copies, waits for them, and re-layouts, column_step(): diag_entry = lax.dynamic_slice_in_dim(gram_row, column, 1, 1)  18.8 us
    psum x1, blocking collectives, local(): gram_cross = lax.psum(local_cross, 'cross')  12.7 us

profile of v3, /device:TPU:1, one launch (start us, length us, event | category | flops | bytes accessed | tf_op | source)
XLA Modules:
  0.0 557.8 jit_solution(10372697452723228785)
XLA Ops:
  1.4 5.9 %fusion.9 = f32[32,32,256]{2,0,1:T(8,128)S(1)} fusion(bf16[32,256,512]{2,1,0:T(8,128)(2,1)} %param.6, bf16[32,512]{1,0:T(8,128)(2,1)S(1)} %copy-done), kind=kOutput, calls=%fused_computation.12 | convolution fusion | flops 268435456 | bytes 9469952 | tf_op jit(solution)/shard_map/dot_general | solution.py:26
  7.3 1.2 fusion.7
  8.5 327.1 %psum.21 = f32[32,32]{1,0:T(8,128)S(1)} all-reduce(f32[32,32]{1,0:T(8,128)S(1)} %bitcast.36), channel_id=1, replica_groups=mesh['roll'=4,'mach'=16,'cross'=4] {'mach','cross'}, use_global_device_ids=true, to_apply=%region_2.0 | all-reduce | flops 1024 | bytes 8192 | tf_op jit(solution)/shard_map/psum | solution.py:38
  335.7 56.2 %psum.22 = f32[32,32]{1,0:T(8,128)S(1)} all-reduce(f32[32,32]{1,0:T(8,128)S(1)} %fusion.12), channel_id=1, replica_groups=mesh['roll'=4,'mach'=16,'cross'=4] {'mach'}, use_global_device_ids=true, to_apply=%region_0.0 | all-reduce | flops 1024 | bytes 8192 | tf_op jit(solution)/shard_map/psum | solution.py:39
  392.0 12.7 %psum.23 = f32[32,32]{1,0:T(8,128)S(1)} all-reduce(f32[32,32]{1,0:T(8,128)S(1)} %fusion.13), channel_id=1, replica_groups=mesh['roll'=4,'mach'=16,'cross'=4] {'cross'}, use_global_device_ids=true, to_apply=%region_1.0 | all-reduce | flops 1024 | bytes 8192 | tf_op jit(solution)/shard_map/psum | solution.py:40
  404.7 45.2 %while.16 = (s32[]{:T(128)}, f32[32,32]{1,0:T(8,128)S(1)}, f32[32,32]{1,0:T(8,128)S(1)}, f32[32,32]{1,0:T(8,128)S(1)}, s32[]{:T(128)}, /*index=5*/s32[]{:T(128)}, s32[]{:T(128)}) while((s32[]{:T(128)}, f32[32,32]{1,0:T(8,128)S(1)}, f32[32,32]{1,0:T(8,128)S(1)}, f32[32,32]{1,0:T(8,128)S(1)}, s32[]{:T(128)}, /*index=5*/s32[]{:T(128)}, ...), condition=%wide.region_4.0_spmd, body=%wide.region_3.0_spmd.sunk | while | flops 12419 | bytes 19449 | solution.py:19
  405.3 0.8 fusion.26
  406.7 0.8 fusion.26
  408.1 0.8 fusion.26
  409.6 0.8 fusion.26
  411.0 0.8 fusion.26
  412.4 0.8 fusion.26
  413.8 0.8 fusion.26
  415.2 0.8 fusion.26
  416.6 0.8 fusion.26
  418.0 0.8 fusion.26
  419.4 0.8 fusion.26
  420.8 0.8 fusion.26
  422.3 0.8 fusion.26
  423.7 0.8 fusion.26
  425.1 0.8 fusion.26
  426.5 0.8 fusion.26
  429.3 0.8 fusion.26
  430.7 0.8 fusion.26
  432.1 0.8 fusion.26
  433.6 0.8 fusion.26
  435.0 0.8 fusion.26
  436.4 0.8 fusion.26
  437.8 0.8 fusion.26
  439.2 0.8 fusion.26
  449.9 1.3 fusion.5
  451.2 105.9 %all-gather = f32[512,256]{1,0:T(8,128)S(1)} all-gather(f32[32,256]{1,0:T(8,128)S(1)} %bitcast.35), channel_id=2, replica_groups=mesh['roll'=4,'mach'=16,'cross'=4] {'roll','cross'}, dimensions={0}, use_global_device_ids=true | all-gather | bytes 557056 | tf_op jit(solution)/shard_map/all_gather | solution.py:44
  (86 shorter events, 27.6 us)
Async XLA Ops:
  0.6 0.8 copy-start
  0.6 404.1 %copy-start.2 = (f32[32,32]{1,0:T(8,128)S(1)}, f32[32,32]{1,0:T(8,128)}, u32[]{:S(2)}) copy-start(f32[32,32]{1,0:T(8,128)} %param.7) | copy-start | bytes 12292
  0.7 6.6 %copy-start.3 = (bf16[32,256]{1,0:T(8,128)(2,1)S(1)}, bf16[32,256]{1,0:T(8,128)(2,1)}, u32[]{:S(2)}) copy-start(bf16[32,256]{1,0:T(8,128)(2,1)} %param.8) | copy-start | bytes 49156
  449.9 107.9 %copy-start.1 = (f32[32,32]{1,0:T(8,128)}, f32[32,32]{1,0:T(8,128)S(1)}, u32[]{:S(2)}) copy-start(f32[32,32]{1,0:T(8,128)S(1)} %get-tuple-element.124) | copy-start | bytes 12292
